TPU v7x, 32 devices: a whole 2x2x4 slice. The times are simulated.
32 devices in a mesh: shard: 4 (over y, core), rep: 8 (over z, x).
Axes of the slice: x: 2, y: 2, z: 4, core: 2. Of those that a mesh axis runs over, the one named last changes fastest.
Arguments:
- tokens: bfloat16 [8, 512, 768], P('rep', 'shard'), may hold values from -6 to 6
- gain_one: bfloat16 [768], P('shard'), may hold values from 0.5 to 1.5
- qkv_weight: bfloat16 [768, 2304], P('shard'), may hold values from -6 to 6
- out_weight: bfloat16 [768, 768], P('shard'), may hold values from -2.5 to 2.5
- gain_two: bfloat16 [768], P('shard'), may hold values from 0.5 to 1.5
- in_weight: bfloat16 [768, 2304], P('shard'), may hold values from -0.21875 to 0.21875
- down_weight: bfloat16 [1152, 768], P('shard'), may hold values from -0.1875 to 0.1875
- grad_output: bfloat16 [8, 512, 768], P('rep', 'shard'), may hold values from -6 to 6
Outputs:
- output: bfloat16 [8, 512, 768], P('rep', 'shard')
- grad_tokens: float32 [8, 512, 768], P('rep', 'shard')
- grad_gain_one: float32 [768], P('shard')
- grad_qkv: float32 [768, 2304], P('shard')
- grad_out: float32 [768, 768], P('shard')
- grad_gain_two: float32 [768], P('shard')
- grad_in: float32 [768, 2304], P('shard')
- grad_down: float32 [1152, 768], P('shard')
All inputs are finite; a program needn't handle non-finite values.
Results may differ from a plain program's by a relative error of at most 0.02.
Values may be sent and summed in bfloat16 or wider, within the bound.
A program may use at most 128 MiB of HBM per device.

v0:
```python
import functools

import jax
import jax.numpy as jnp
from jax import lax
from jax.experimental import pallas as pl
from jax.experimental.pallas import tpu as pltpu
from jax.sharding import PartitionSpec as P

HEAD_DIM = 64
EPSILON = 1e-05
THETA = 160000.0
SQRT_HALF = 0.7071067811865476
INV_SQRT_TAU = 0.3989422804014327
MESH_ID = pl.DeviceIdType.MESH
LANES = 128
VMEM = pl.BlockSpec(memory_space=pltpu.VMEM)


def layer_norm(values, gain):
    mean_row = jnp.mean(values, axis=-1, keepdims=True)
    centred = values - mean_row
    variance = jnp.mean(centred * centred, axis=-1, keepdims=True)
    inverse = lax.rsqrt(variance + EPSILON)
    normed = centred * inverse
    return (normed, inverse, normed * gain.astype(jnp.float32))


def norm_backward(grad_out, normed, inverse, gain):
    grad_normed = grad_out * gain.astype(jnp.float32)
    gain_grad = jnp.sum(grad_out * normed, axis=0)
    first = jnp.mean(grad_normed, axis=-1, keepdims=True)
    second = jnp.mean(grad_normed * normed, axis=-1, keepdims=True)
    return (inverse * (grad_normed - first - normed * second), gain_grad)


def rotary_tables(count, head_dim):
    half = head_dim // 2
    positions = jnp.arange(count, dtype=jnp.int32)
    freq = THETA ** (-jnp.arange(half, dtype=jnp.float32) * 2.0 / head_dim)
    angles = positions.astype(jnp.float32)[:, None] * freq[None, :]
    angles = jnp.concatenate([angles, angles], axis=-1)
    return (jnp.cos(angles)[None], jnp.sin(angles)[None])


def rotate_half(values):
    half = values.shape[-1] // 2
    return jnp.concatenate([-values[..., half:], values[..., :half]], axis=-1)


def gelu_pair(inner):
    cdf = 0.5 * (1.0 + jax.scipy.special.erf(inner * SQRT_HALF))
    return (inner * cdf, cdf + inner * jnp.exp(-0.5 * inner * inner) * INV_SQRT_TAU)


def outer_sum(left, right):
    return lax.dot_general(
        left, right, (((0,), (0,)), ((), ())), preferred_element_type=jnp.float32
    )


def times_transposed(left, weight):
    return lax.dot_general(
        left, weight, (((1,), (1,)), ((), ())), preferred_element_type=jnp.float32
    )


def flip(index, bit):
    return index + bit * (1 - 2 * ((index // bit) % 2))


def remote(src, dst, send, recv, axis, target):
    return pltpu.make_async_remote_copy(
        src_ref=src,
        dst_ref=dst,
        send_sem=send,
        recv_sem=recv,
        device_id={axis: target},
        device_id_type=MESH_ID,
    )


def greet(partners):
    barrier = pltpu.get_barrier_semaphore()
    for axis, target in partners:
        pl.semaphore_signal(barrier, inc=1, device_id={axis: target}, device_id_type=MESH_ID)
    pl.semaphore_wait(barrier, len(partners))


def shard_partners(me):
    return [("shard", flip(me, 1)), ("shard", flip(me, 2)), ("shard", flip(flip(me, 1), 2))]


def gather_kernel(gathered, kinds, *refs):
    total = gathered + len(kinds)
    ins, outs = refs[:total], refs[total : 2 * total]
    packed = refs[2 * total : 2 * total + len(kinds)]
    send, recv, local_sem = refs[2 * total + len(kinds) :]
    me = lax.axis_index("shard")
    partners = shard_partners(me)
    greet(partners)
    (_, core), (_, chip), (_, diagonal) = partners
    pending = []
    sent = []
    for i in range(gathered):
        far = remote(ins[i], outs[i].at[me], send.at[i, 0], recv.at[i, 0], "shard", chip)
        far.start()
        near = remote(ins[i], outs[i].at[me], send.at[i, 1], recv.at[i, 1], "shard", core)
        near.start()
        own = pltpu.make_async_copy(ins[i], outs[i].at[me], local_sem.at[i])
        own.start()
        pending.append((far, near, own))
    for i in range(gathered, total):
        source, buffer, kind_count = ins[i], packed[i - gathered], kinds[i - gathered]
        blocks, _, columns = buffer.shape
        size = columns // kind_count
        for j in range(blocks):
            for kind in range(kind_count):
                start = (kind * blocks + j) * size
                buffer[j, :, kind * size : (kind + 1) * size] = source[:, start : start + size]
        copies = []
        for k, target in enumerate((chip, diagonal, core)):
            copy = remote(
                buffer.at[target], outs[i].at[me], send.at[i, k], recv.at[i, k], "shard", target
            )
            copy.start()
            copies.append(copy)
        own = pltpu.make_async_copy(buffer.at[me], outs[i].at[me], local_sem.at[i])
        own.start()
        sent.append((copies, own))
    for i in range(gathered):
        pending[i][0].wait_recv()
        relay = remote(
            outs[i].at[chip], outs[i].at[chip], send.at[i, 2], recv.at[i, 2], "shard", core
        )
        relay.start()
        pending[i] = pending[i] + (relay,)
    for far, near, own, relay in pending:
        far.wait_send()
        near.wait()
        own.wait()
        relay.wait()
    for copies, own in sent:
        for copy in copies:
            copy.wait()
        own.wait()


def gather(collective, gathered, swapped, kinds, n_shard):
    arrays = tuple(gathered) + tuple(swapped)
    shapes = [jax.ShapeDtypeStruct((n_shard,) + a.shape, a.dtype) for a in gathered]
    blocks = [
        jax.ShapeDtypeStruct((n_shard, a.shape[0], a.shape[1] // n_shard), a.dtype)
        for a in swapped
    ]
    return pl.pallas_call(
        functools.partial(gather_kernel, len(gathered), tuple(kinds)),
        out_shape=tuple(shapes + blocks),
        in_specs=[VMEM] * len(arrays),
        out_specs=tuple([VMEM] * len(arrays)),
        scratch_shapes=[pltpu.VMEM(b.shape, b.dtype) for b in blocks]
        + [
            pltpu.SemaphoreType.DMA((len(arrays), 3)),
            pltpu.SemaphoreType.DMA((len(arrays), 3)),
            pltpu.SemaphoreType.DMA((len(arrays),)),
        ],
        compiler_params=pltpu.CompilerParams(collective_id=collective, has_side_effects=True),
    )(*arrays)


def scatter_kernel(total, *refs):
    ins, outs = refs[:total], refs[total : 2 * total]
    near_buf, out_buf, far_buf, send, recv = refs[2 * total :]
    me = lax.axis_index("shard")
    partners = shard_partners(me)[:2]
    greet(partners)
    (_, core), (_, chip) = partners
    diagonal = flip(core, 2)
    first, second, third = [], [], []
    for i in range(total):
        a = remote(
            ins[i].at[diagonal], near_buf.at[i, 0], send.at[i, 0], recv.at[i, 0], "shard", core
        )
        a.start()
        b = remote(ins[i].at[core], near_buf.at[i, 1], send.at[i, 1], recv.at[i, 1], "shard", core)
        b.start()
        first.append(a)
        second.append(b)
    for i in range(total):
        first[i].wait_recv()
        out_buf[i] = (
            ins[i][chip].astype(jnp.float32) + near_buf[i, 0].astype(jnp.float32)
        ).astype(jnp.bfloat16)
        c = remote(out_buf.at[i], far_buf.at[i], send.at[i, 2], recv.at[i, 2], "shard", chip)
        c.start()
        third.append(c)
    for i in range(total):
        second[i].wait_recv()
        outs[i][...] = ins[i][me].astype(jnp.float32) + near_buf[i, 1].astype(jnp.float32)
    for i in range(total):
        third[i].wait_recv()
        outs[i][...] += far_buf[i].astype(jnp.float32)
    for i in range(total):
        first[i].wait_send()
        second[i].wait_send()
        third[i].wait_send()


def scatter(collective, arrays):
    total = len(arrays)
    block = arrays[0].shape[1:]
    return pl.pallas_call(
        functools.partial(scatter_kernel, total),
        out_shape=tuple([jax.ShapeDtypeStruct(block, jnp.float32)] * total),
        in_specs=[VMEM] * total,
        out_specs=tuple([VMEM] * total),
        scratch_shapes=[
            pltpu.VMEM((total, 2) + block, jnp.bfloat16),
            pltpu.VMEM((total,) + block, jnp.bfloat16),
            pltpu.VMEM((total,) + block, jnp.bfloat16),
            pltpu.SemaphoreType.DMA((total, 3)),
            pltpu.SemaphoreType.DMA((total, 3)),
        ],
        compiler_params=pltpu.CompilerParams(collective_id=collective, has_side_effects=True),
    )(*arrays)


def halves(order, me):
    length = 1 << len(order)
    offset = 0
    plan = []
    for bit in order:
        length //= 2
        side = (me // bit) % 2
        plan.append((bit, offset + side * length, offset + (1 - side) * length, length))
        offset = offset + side * length
    return plan


class Stream:
    def __init__(self, buffer, base, rows, order, swap):
        self.buffer, self.base, self.rows, self.order, self.swap = buffer, base, rows, order, swap


def streams_of(buffer, rows, n_rep, swap):
    tiles = -(-rows // (16 * n_rep))
    low_first = tuple(1 << i for i in range(n_rep.bit_length() - 1))
    orders = (low_first, low_first[1::-1] + low_first[2:])
    streams = []
    base = 0
    for share, order in zip((tiles - tiles // 2, tiles // 2), orders):
        if share:
            streams.append(Stream(buffer, base, 16 * share, order, swap))
            base += 16 * share * n_rep
    return streams, base


class RepSum:
    def __init__(self, streams, acc, box, res, sems):
        self.streams, self.acc, self.box, self.res = streams, acc, box, res
        self.send, self.recv, self.swap_send, self.swap_recv, self.local_sem = sems
        self.rep = lax.axis_index("rep")
        self.me = lax.axis_index("shard")
        self.group = shard_partners(self.me)
        self.steps = len(streams[0].order)
        self.plans = [halves(stream.order, self.rep) for stream in streams]
        self.started = [[] for _ in streams]

    def at(self, ref, i, piece, length, lead=None):
        stream = self.streams[i]
        start = stream.base + piece * stream.rows
        if not isinstance(start, int):
            start = pl.multiple_of(start, 16)
        rows = pl.ds(start, length * stream.rows)
        if not stream.swap:
            return ref.at[rows]
        return ref.at[slice(None) if lead is None else lead, rows]

    def begin(self, i, k):
        stream, plan, steps = self.streams[i], self.plans[i], self.steps
        acc, box, res = (refs[stream.buffer] for refs in (self.acc, self.box, self.res))
        if k < steps:
            bit, _, sent, length = plan[k]
            copies = [
                remote(
                    self.at(acc, i, sent, length),
                    self.at(box, i, length, length),
                    self.send.at[i, k],
                    self.recv.at[i, k],
                    "rep",
                    flip(self.rep, bit),
                )
            ]
        elif k == steps:
            mine = plan[-1][1]
            if not stream.swap:
                copies = [
                    pltpu.make_async_copy(
                        self.at(acc, i, mine, 1), self.at(res, i, mine, 1), self.local_sem.at[i]
                    )
                ]
            else:
                target_block = self.at(res, i, mine, 1, self.me)
                copies = [
                    remote(
                        self.at(acc, i, mine, 1, target),
                        target_block,
                        self.swap_send.at[i, j],
                        self.swap_recv.at[i, j],
                        "shard",
                        target,
                    )
                    for j, (_, target) in enumerate(self.group)
                ]
                copies.append(
                    pltpu.make_async_copy(
                        self.at(acc, i, mine, 1, self.me), target_block, self.local_sem.at[i]
                    )
                )
        else:
            bit, kept, _, length = plan[2 * steps - k]
            region = self.at(res, i, kept, length)
            copies = [
                remote(
                    region,
                    region,
                    self.send.at[i, k - 1],
                    self.recv.at[i, k - 1],
                    "rep",
                    flip(self.rep, bit),
                )
            ]
        for copy in copies:
            copy.start()
        self.started[i].append(copies)

    def finish(self, i, k):
        copies, stream = self.started[i][k], self.streams[i]
        if k == self.steps:
            for copy in copies:
                copy.wait()
            return
        copies[0].wait_recv()
        if k > self.steps:
            return
        acc, box = self.acc[stream.buffer], self.box[stream.buffer]
        _, kept, _, length = self.plans[i][k]
        blocks = range(acc.shape[0]) if stream.swap else (None,)

        @pl.loop(0, length * stream.rows // 16)
        def _(p):
            to = pl.ds(pl.multiple_of(stream.base + kept * stream.rows + 16 * p, 16), 16)
            of = pl.ds(pl.multiple_of(stream.base + length * stream.rows + 16 * p, 16), 16)
            for block in blocks:
                x, y = ((to,), (of,)) if block is None else ((block, to), (block, of))
                acc[x] = (acc[x].astype(jnp.float32) + box[y].astype(jnp.float32)).astype(
                    jnp.bfloat16
                )

    def begin_all(self, chosen):
        for i in chosen:
            self.begin(i, 0)

    def step(self, chosen, k):
        for i in chosen:
            self.finish(i, k)
            if k < 2 * self.steps:
                self.begin(i, k + 1)

    def close(self, chosen):
        for i in chosen:
            for k in range(2 * self.steps + 1):
                if k != self.steps:
                    self.started[i][k][0].wait_send()


def pack_columns(source, target, gain):
    blocks, rows, columns = source.shape
    full, rest = divmod(columns, LANES)
    for s in range(blocks):
        for j in range(full):
            target[s, j * rows : (j + 1) * rows] = source[s, :, j * LANES : (j + 1) * LANES]
        at = full * rows
        if rest:
            half = rows // 2
            target[s, at : at + half, :rest] = source[s, :half, full * LANES :]
            target[s, at : at + half, rest:] = source[s, half:, full * LANES :]
            at += half
        target[s, at : at + 16] = gain[s]
        if at + 16 < target.shape[1]:
            target[s, at + 16 :] = jnp.zeros((target.shape[1] - at - 16, LANES), target.dtype)


def unpack_columns(source, out, gain_out, kinds):
    blocks = source.shape[0]
    rows, width = out.shape
    columns = width // blocks
    size = columns // kinds
    full, rest = divmod(columns, LANES)
    half = rows // 2
    at = full * rows
    gain = jnp.zeros((16, LANES), jnp.float32)
    for t in range(blocks):
        parts = [source[t, j * rows : (j + 1) * rows] for j in range(full)]
        end = at
        if rest:
            tail = source[t, at : at + half]
            parts.append(jnp.concatenate([tail[:, :rest], tail[:, rest:]], axis=0))
            end += half
        block = jnp.concatenate([p.astype(jnp.float32) for p in parts], axis=1)
        gain += source[t, end : end + 16].astype(jnp.float32)
        for kind in range(kinds):
            start = (kind * blocks + t) * size
            out[:, start : start + size] = block[:, kind * size : (kind + 1) * size]
    gain_out[...] = gain


def pack_rows(sources, target):
    tall = sum(source.shape[0] for source in sources)
    at = 0
    for source in sources:
        rows = source.shape[0]
        for j in range(source.shape[1] // LANES):
            target[j * tall + at : j * tall + at + rows] = source[:, j * LANES : (j + 1) * LANES]
        at += rows
    end = tall * sources[0].shape[1] // LANES
    if end < target.shape[0]:
        target[end:] = jnp.zeros((target.shape[0] - end, LANES), target.dtype)


def unpack_rows(source, outs):
    tall = sum(out.shape[0] for out in outs)
    at = 0
    for out in outs:
        rows = out.shape[0]
        for j in range(out.shape[1] // LANES):
            out[:, j * LANES : (j + 1) * LANES] = source[
                j * tall + at : j * tall + at + rows
            ].astype(jnp.float32)
        at += rows


def column_rows(shape):
    _, rows, columns = shape
    return rows * columns // LANES + 16


def sum_kernel(streams, qkv, gain1, win, gain2, gout, gdown, *refs):
    o_qkv, o_gain1, o_in, o_gain2, o_out, o_down = refs[:6]
    acc, box, res = refs[6:9], refs[9:12], refs[12:15]
    pack_rows((gout, gdown), acc[0])
    pack_columns(win, acc[1], gain2)
    pack_columns(qkv, acc[2], gain1)
    rep_sum = RepSum(streams, acc, box, res, refs[15:])
    bits = sorted(streams[0].order)
    greet([("rep", flip(rep_sum.rep, bit)) for bit in bits] + rep_sum.group)
    chosen = range(len(streams))
    rep_sum.begin_all(chosen)
    for k in range(2 * rep_sum.steps + 1):
        rep_sum.step(chosen, k)
    unpack_rows(res[0], (o_out, o_down))
    unpack_columns(res[1], o_in, o_gain2, 2)
    unpack_columns(res[2], o_qkv, o_gain1, 3)
    rep_sum.close(chosen)


def sum_over_rep(collective, n_rep, qkv, gain1, win, gain2, gout, gdown):
    b16, f32 = jnp.bfloat16, jnp.float32
    n_shard, part, columns = qkv.shape
    width = columns * n_shard
    plain_rows = (gout.shape[0] + gdown.shape[0]) * gout.shape[1] // LANES
    streams, shapes = [], []
    for i, (rows, swap) in enumerate(
        ((plain_rows, False), (column_rows(win.shape), True), (column_rows(qkv.shape), True))
    ):
        more, padded = streams_of(i, rows, n_rep, swap)
        streams += more
        shapes.append((n_shard, padded, LANES) if swap else (padded, LANES))
    steps = len(streams[0].order)
    count = len(streams)
    outs = [(part, width), (16, LANES), (part, win.shape[2] * n_shard), (16, LANES)]
    outs += [gout.shape, gdown.shape]
    return pl.pallas_call(
        functools.partial(sum_kernel, streams),
        out_shape=tuple(jax.ShapeDtypeStruct(shape, f32) for shape in outs),
        in_specs=[VMEM] * 6,
        out_specs=tuple([VMEM] * 6),
        scratch_shapes=[pltpu.VMEM(shape, b16) for shape in shapes * 3]
        + [
            pltpu.SemaphoreType.DMA((count, 2 * steps)),
            pltpu.SemaphoreType.DMA((count, 2 * steps)),
            pltpu.SemaphoreType.DMA((count, 3)),
            pltpu.SemaphoreType.DMA((count, 3)),
            pltpu.SemaphoreType.DMA((count,)),
        ],
        compiler_params=pltpu.CompilerParams(collective_id=collective, has_side_effects=True),
    )(qkv, gain1, win, gain2, gout, gdown)


def local(
    n_shard, n_rep, tokens, gain_one, qkv_weight, out_weight, gain_two, in_weight, down_weight,
    grad_output
):
    tok_dev, width = tokens.shape[1:]
    part = width // n_shard
    heads = part // HEAD_DIM
    hidden = down_weight.shape[0]
    count = tok_dev * n_shard
    scale = HEAD_DIM ** (-0.5)
    f32, b16 = jnp.float32, jnp.bfloat16
    own_tokens = tokens.reshape(tok_dev, width)
    own_grad = grad_output.reshape(tok_dev, width)

    all_tokens, all_g1, all_g2, all_grad, my_qkv, my_in = gather(
        0,
        (own_tokens, gain_one.reshape(1, part), gain_two.reshape(1, part), own_grad),
        (qkv_weight, in_weight),
        (3, 2),
        n_shard,
    )
    full_g1 = all_g1.reshape(width)
    full_g2 = all_g2.reshape(width)
    my_qkv = my_qkv.reshape(width, 3 * part)
    my_in = my_in.reshape(width, 2 * hidden)
    grad_b = all_grad.reshape(count, width)

    inputs = own_tokens.astype(f32)
    normed_one, inverse_one, _ = layer_norm(inputs, full_g1)
    hidden_one = layer_norm(all_tokens.reshape(count, width).astype(f32), full_g1)[2].astype(b16)
    projected = jnp.dot(hidden_one, my_qkv, preferred_element_type=f32)
    cosine, sine = rotary_tables(count, HEAD_DIM)
    split = projected.reshape(count, 3, heads, HEAD_DIM).transpose(1, 2, 0, 3)
    queries, key_raw = split[0], split[1]
    query_rot = (queries * cosine + rotate_half(queries) * sine).astype(b16)
    key_rot = (key_raw * cosine + rotate_half(key_raw) * sine).astype(b16)
    values = split[2].astype(b16)
    scores = jnp.einsum("hqd,hkd->hqk", query_rot, key_rot, preferred_element_type=f32) * scale
    maxima = jnp.max(scores, axis=-1, keepdims=True)
    expo = jnp.exp(scores - maxima)
    totals = jnp.sum(expo, axis=-1, keepdims=True)
    accum = jnp.einsum("hqk,hkd->hqd", expo.astype(b16), values, preferred_element_type=f32)
    att_heads = (accum / totals).astype(b16)
    attended = att_heads.transpose(1, 0, 2).reshape(count, part)
    partial = jnp.dot(attended, out_weight, preferred_element_type=f32).astype(b16)
    (mixed,) = scatter(1, (partial.reshape(n_shard, tok_dev, width),))
    resid = inputs + mixed
    normed_two, inverse_two, scaled_two = layer_norm(resid, full_g2)
    (hidden_two,) = gather(2, (scaled_two.astype(b16),), (), (), n_shard)
    hidden_two = hidden_two.reshape(count, width)
    upper = jnp.dot(hidden_two, my_in, preferred_element_type=f32)
    inner, gate_half = upper[:, :hidden], upper[:, hidden:]
    gelu_value, gelu_slope = gelu_pair(inner)
    act = (gelu_value * gate_half).astype(b16)
    down_part = jnp.dot(act, down_weight, preferred_element_type=f32).astype(b16)
    grad_down = outer_sum(act, grad_b)
    grad_act = times_transposed(grad_b, down_weight)
    grad_upper = jnp.concatenate(
        [grad_act * gate_half * gelu_slope, grad_act * gelu_value], axis=-1
    ).astype(b16)
    grad_in = outer_sum(hidden_two, grad_upper)
    h2_part = times_transposed(grad_upper, my_in).astype(b16)
    down_sum, grad_h2 = scatter(
        3, (down_part.reshape(n_shard, tok_dev, width), h2_part.reshape(n_shard, tok_dev, width))
    )
    output = (resid + down_sum).astype(b16)
    norm_grad_two, grad_gain_two = norm_backward(grad_h2, normed_two, inverse_two, full_g2)
    grad_resid = own_grad.astype(f32) + norm_grad_two
    (resid_b,) = gather(4, (grad_resid.astype(b16),), (), (), n_shard)
    resid_b = resid_b.reshape(count, width)
    grad_out = outer_sum(attended, resid_b)
    grad_att = times_transposed(resid_b, out_weight).astype(b16)
    grad_heads = grad_att.reshape(count, heads, HEAD_DIM).transpose(1, 0, 2)
    delta = jnp.sum(grad_heads.astype(f32) * att_heads.astype(f32), axis=-1, keepdims=True)
    probs = expo / totals
    grad_value = jnp.einsum(
        "hqk,hqd->khd", probs.astype(b16), grad_heads, preferred_element_type=f32
    )
    grad_probs = jnp.einsum("hqd,hkd->hqk", grad_heads, values, preferred_element_type=f32)
    grad_scores = (probs * (grad_probs - delta) * scale).astype(b16)
    grad_qr = jnp.einsum("hqk,hkd->hqd", grad_scores, key_rot, preferred_element_type=f32)
    grad_kr = jnp.einsum("hqk,hqd->hkd", grad_scores, query_rot, preferred_element_type=f32)
    grad_q = (grad_qr * cosine - rotate_half(grad_qr) * sine).transpose(1, 0, 2)
    grad_k = (grad_kr * cosine - rotate_half(grad_kr) * sine).transpose(1, 0, 2)
    grad_projected = jnp.concatenate(
        [g.reshape(count, part) for g in (grad_q, grad_k, grad_value)], axis=-1
    ).astype(b16)
    grad_qkv = outer_sum(hidden_one, grad_projected)
    h1_part = times_transposed(grad_projected, my_qkv).astype(b16)
    (grad_h1,) = scatter(5, (h1_part.reshape(n_shard, tok_dev, width),))
    norm_grad_one, grad_gain_one = norm_backward(grad_h1, normed_one, inverse_one, full_g1)
    grad_tokens = grad_resid + norm_grad_one

    def gain_rows(gain):
        room = -part % LANES
        rows = jnp.pad(gain.reshape(n_shard, part), ((0, 0), (0, room)))
        rows = rows.reshape(n_shard, -1, LANES)
        return jnp.pad(rows, ((0, 0), (0, 16 - rows.shape[1]), (0, 0))).astype(b16)

    sum_qkv, sum_g1, sum_in, sum_g2, sum_out, sum_down = sum_over_rep(
        6,
        n_rep,
        grad_qkv.astype(b16).reshape(n_shard, part, -1),
        gain_rows(grad_gain_one),
        grad_in.astype(b16).reshape(n_shard, part, -1),
        gain_rows(grad_gain_two),
        grad_out.astype(b16),
        grad_down.astype(b16),
    )
    return (
        output.reshape(1, tok_dev, width),
        grad_tokens.reshape(1, tok_dev, width),
        sum_g1.reshape(-1)[:part],
        sum_qkv,
        sum_out,
        sum_g2.reshape(-1)[:part],
        sum_in,
        sum_down,
    )


def solution(mesh):
    in_specs = (
        P("rep", "shard", None),
        P("shard"),
        P("shard", None),
        P("shard", None),
        P("shard"),
        P("shard", None),
        P("shard", None),
        P("rep", "shard", None),
    )
    out_specs = (
        P("rep", "shard", None),
        P("rep", "shard", None),
        P("shard"),
        P("shard", None),
        P("shard", None),
        P("shard"),
        P("shard", None),
        P("shard", None),
    )
    body = functools.partial(local, mesh.shape["shard"], mesh.shape["rep"])
    return jax.shard_map(body, mesh=mesh, in_specs=in_specs, out_specs=out_specs, check_vma=False)
```

profile of v0, /device:TPU:0, one launch (start us, length us, event | category | flops | bytes accessed | tf_op | source)
XLA Modules:
  0.0 231.9 jit_solution(2405898123812935788)
XLA Ops:
  0.6 1.1 convert_reduce_fusion.1
  1.8 1.2 reshape.284.refs_1_
  3.0 1.2 reshape.285.refs_2_
  4.3 0.9 fusion.46
  5.2 37.6 %shard_map.143 = (bf16[4,128,768]{2,1,0:T(8,128)(2,1)}, bf16[4,1,192]{2,1,0:T(2,128)(2,1)}, bf16[4,1,192]{2,1,0:T(2,128)(2,1)}, bf16[4,128,768]{2,1,0:T(8,128)(2...) custom-call(bf16[128,768]{1,0:T(8,128)(2,1)} %bitcast.112, bf16[1,192]{1,0:T(2,128)(2,1)} %reshape.284.refs_1_, ...), custom_call_target="tpu_custom_call" | custom-call | tf_op jit(solution)/shard_map/pallas_call | solution.py:156
  42.8 0.8 convert_reduce_fusion.2
  43.7 1.3 convert_reduce_fusion
  45.0 1.5 multiply_reduce_fusion.1
  46.6 1.2 fusion.7
  48.1 1.5 copy.16
  49.6 0.7 convolution_bitcast_fusion
  50.5 0.7 copy-done.9
  51.5 0.6 multiply_reduce_fusion
  52.7 1.1 copy-done.1
  53.8 1.4 fusion.42
  55.2 1.3 convolution_convert_fusion.5
  56.5 10.6 %shard_map.144 = f32[128,768]{1,0:T(8,128)} custom-call(bf16[4,128,768]{2,1,0:T(8,128)(2,1)} %bitcast.116), custom_call_target="tpu_custom_call" | custom-call | tf_op jit(solution)/shard_map/pallas_call | solution.py:212
  67.1 1.2 fusion.58
  68.5 0.8 multiply_convert_fusion.4.refs_0_
  69.3 10.2 %shard_map.145 = bf16[4,128,768]{2,1,0:T(8,128)(2,1)} custom-call(bf16[128,768]{1,0:T(8,128)(2,1)} %multiply_convert_fusion.4.refs_0_), custom_call_target="tpu_custom_call" | custom-call | tf_op jit(solution)/shard_map/pallas_call | solution.py:156
  79.4 2.2 fusion.59
  81.7 0.6 fusion.21
  82.3 1.2 convolution_convert_fusion.6.gdown
  83.5 1.7 convolution_convert_fusion.3
  85.2 1.5 convolution_convert_fusion
  86.7 2.2 copy.23
  88.9 1.5 convolution_convert_fusion.4
  90.4 15.2 %shard_map.146 = (f32[128,768]{1,0:T(8,128)}, f32[128,768]{1,0:T(8,128)}) custom-call(bf16[4,128,768]{2,1,0:T(8,128)(2,1)} %bitcast.131, bf16[4,128,768]{2,1,0:T(8,128)(2,1)} %bitcast.129), custom_call_target="tpu_custom_call" | custom-call | tf_op jit(solution)/shard_map/pallas_call | solution.py:212
  105.6 1.2 multiply_reduce_fusion.2
  107.0 2.1 fusion.57
  109.7 10.2 %shard_map.147 = bf16[4,128,768]{2,1,0:T(8,128)(2,1)} custom-call(bf16[128,768]{1,0:T(8,128)(2,1)} %get-tuple-element.42.refs_0_), custom_call_target="tpu_custom_call" | custom-call | tf_op jit(solution)/shard_map/pallas_call | solution.py:156
  119.9 2.3 %convolution_convert_fusion.7.gout = bf16[192,768]{1,0:T(8,128)(2,1)} fusion(bf16[512,192]{0,1:T(8,128)(2,1)S(1)} %bitcast.121, bf16[512,768]{1,0:T(8,128)(2,1)} %bitcast.110), kind=kOutput, calls=%fused_computation.26 | convolution fusion | flops 151142400 | bytes 1277952 | tf_op jit(solution)/shard_map/dot_general | solution.py:57
  122.2 1.5 convolution_convert_fusion.8
  123.9 0.8 fusion.12
  124.6 1.0 multiply_convert_fusion
  128.0 1.7 convolution_convert_fusion.2
  129.7 0.6 convolution_convert_fusion.1
  130.3 10.6 %shard_map.148 = f32[128,768]{1,0:T(8,128)} custom-call(bf16[4,128,768]{2,1,0:T(8,128)(2,1)} %bitcast.130), custom_call_target="tpu_custom_call" | custom-call | tf_op jit(solution)/shard_map/pallas_call | solution.py:212
  140.9 1.2 fusion.32
  142.2 1.9 fusion.31
  144.8 1.3 copy.22
  146.1 76.9 %shard_map.149 = (f32[192,2304]{1,0:T(8,128)}, f32[16,128]{1,0:T(8,128)}, f32[192,2304]{1,0:T(8,128)}, f32[16,128]{1,0:T(8,128)}, f32[192,768]{1,0:T(8,128)}, /*index=5*/f32[288,768]{1,0:T(8,128)}) custom-call(bf16[4,192,576]{2,1,0:T(8,128)(2,1)} %bitcast.114, bf16[4,16,128]{2,1,0:T(8,128)(2,1)} %pad.19.gain1, bf16[4,192,576]{2,1,0:T(8,128)(2,1)} %bitcast.113, ...), custom_call_target="tpu_custom_call" | custom-call | tf_op jit(solution)/shard_map/pallas_call | solution.py:483
  223.0 1.2 slice.74
  224.2 1.2 slice.75
  225.5 2.9 %copy.34 = f32[192,2304]{1,0:T(8,128)} copy(f32[192,2304]{1,0:T(8,128)} %get-tuple-element.88) | data formatting | bytes 3538944
  228.4 0.8 copy.35
  229.2 1.2 copy.36
  231.0 0.9 copy.37
  (72 shorter events, 6.1 us)
Async XLA Ops:
  0.6 81.0 %copy-start = (bf16[288,768]{1,0:T(8,128)(2,1)S(1)}, bf16[288,768]{1,0:T(8,128)(2,1)}, u32[]{:S(2)}) copy-start(bf16[288,768]{1,0:T(8,128)(2,1)} %param.14) | copy-start | bytes 1327108
  42.8 3.8 %copy-start.3 = (bf16[4,128,768]{2,1,0:T(8,128)(2,1)S(1)}, bf16[4,128,768]{2,1,0:T(8,128)(2,1)}, u32[]{:S(2)}) copy-start(bf16[4,128,768]{2,1,0:T(8,128)(2,1)} %get-tuple-element.22) | copy-start | bytes 2359300
  50.3 0.9 copy-start.9
  50.3 1.0 copy-start.11
  52.1 1.7 copy-start.1
  53.8 1.4 copy-start.8
  55.2 11.9 %copy-start.4 = (bf16[1,128,768]{2,1,0:T(8,128)(2,1)S(1)}, bf16[1,128,768]{2,1,0:T(8,128)(2,1)}, u32[]{:S(2)}) copy-start(bf16[1,128,768]{2,1,0:T(8,128)(2,1)} %param.8) | copy-start | bytes 589828
  79.4 2.2 copy-start.17
  81.7 1.8 copy-start.14
  83.5 1.7 copy-start.5
  109.7 14.1 %copy-start.7 = (f32[3,512,64]{1,2,0:T(8,128)S(1)}, f32[3,512,64]{1,2,0:T(8,128)}, u32[]{:S(2)}) copy-start(f32[3,512,64]{1,2,0:T(8,128)} %get-tuple-element.74) | copy-start | bytes 1179652
  119.9 4.0 %copy-start.2 = (f32[3,512,512]{1,2,0:T(8,128)S(1)}, f32[3,512,512]{1,2,0:T(8,128)}, u32[]{:S(2)}) copy-start(f32[3,512,512]{1,2,0:T(8,128)} %copy-done.1) | copy-start | bytes 9437188
  126.3 0.9 copy-start.10
  126.3 1.0 copy-start.12
  126.7 1.2 copy-start.13
  128.0 1.7 copy-start.16
  225.5 3.0 %copy-start.18 = (f32[192,768]{1,0:T(8,128)S(1)}, f32[192,768]{1,0:T(8,128)}, u32[]{:S(2)}) copy-start(f32[192,768]{1,0:T(8,128)} %get-tuple-element.89) | copy-start | bytes 1769476
  225.5 3.8 %copy-start.6 = (f32[192,2304]{1,0:T(8,128)S(1)}, f32[192,2304]{1,0:T(8,128)}, u32[]{:S(2)}) copy-start(f32[192,2304]{1,0:T(8,128)} %get-tuple-element.91) | copy-start | bytes 5308420
  229.2 1.8 copy-start.15
where the time goes:
time: 233 us; the launch traced here: 232 us
  Pallas kernels  171 us (73%)
  matrix products  21.6 us (9%)
  local copies, waits for them, and re-layouts  21 us (9%)
  other arithmetic  17.1 us (7%)
    pallas_call x1, Pallas kernels, sum_over_rep(): pl.pallas_call(functools.partial(sum_kernel, streams), out_shape=tuple((j...  76.9 us
    pallas_call x3, Pallas kernels, gather(): pl.pallas_call(functools.partial(gather_kernel, len(gathered), tuple(kind...  57.9 us
    pallas_call x3, Pallas kernels, scatter(): pl.pallas_call(functools.partial(scatter_kernel, total), out_shape=tuple(...  36.3 us
    unnamed x42, local copies, waits for them, and re-layouts  9.38 us
    dot_general x4, matrix products, outer_sum(): lax.dot_general(left, right, (((0,), (0,)), ((), ())), preferred_element_...  5.64 us
    dot_general x4, matrix products, times_transposed(): lax.dot_general(left, weight, (((1,), (1,)), ((), ())), preferred_element...  5.59 us

commit v1 on v0

--- a/solution.py
+++ b/solution.py
@@ -91,18 +91,20 @@
     return [("shard", flip(me, 1)), ("shard", flip(me, 2)), ("shard", flip(flip(me, 1), 2))]
 
 
-def gather_kernel(gathered, kinds, *refs):
+def gather_kernel(gathered, kinds, relays, *refs):
     total = gathered + len(kinds)
     ins, outs = refs[:total], refs[total : 2 * total]
     packed = refs[2 * total : 2 * total + len(kinds)]
     send, recv, local_sem = refs[2 * total + len(kinds) :]
     me = lax.axis_index("shard")
     partners = shard_partners(me)
-    greet(partners)
+    rep = lax.axis_index("rep")
+    bits = [1 << b for b in range(relays)] if kinds else []
+    greet(partners + [("rep", flip(rep, bit)) for bit in bits])
     (_, core), (_, chip), (_, diagonal) = partners
     pending = []
-    sent = []
-    for i in range(gathered):
+
+    def begin(i):
         far = remote(ins[i], outs[i].at[me], send.at[i, 0], recv.at[i, 0], "shard", chip)
         far.start()
         near = remote(ins[i], outs[i].at[me], send.at[i, 1], recv.at[i, 1], "shard", core)
@@ -110,58 +112,100 @@
         own = pltpu.make_async_copy(ins[i], outs[i].at[me], local_sem.at[i])
         own.start()
         pending.append((far, near, own))
-    for i in range(gathered, total):
-        source, buffer, kind_count = ins[i], packed[i - gathered], kinds[i - gathered]
-        blocks, _, columns = buffer.shape
-        size = columns // kind_count
-        for j in range(blocks):
-            for kind in range(kind_count):
-                start = (kind * blocks + j) * size
-                buffer[j, :, kind * size : (kind + 1) * size] = source[:, start : start + size]
-        copies = []
-        for k, target in enumerate((chip, diagonal, core)):
-            copy = remote(
-                buffer.at[target], outs[i].at[me], send.at[i, k], recv.at[i, k], "shard", target
-            )
-            copy.start()
-            copies.append(copy)
-        own = pltpu.make_async_copy(buffer.at[me], outs[i].at[me], local_sem.at[i])
-        own.start()
-        sent.append((copies, own))
-    for i in range(gathered):
+
+    def pass_on(i):
         pending[i][0].wait_recv()
         relay = remote(
             outs[i].at[chip], outs[i].at[chip], send.at[i, 2], recv.at[i, 2], "shard", core
         )
         relay.start()
         pending[i] = pending[i] + (relay,)
+
+    late = gathered - 1 if kinds else gathered
+    for i in range(late):
+        begin(i)
+    shared, whole_copies, own_copies = [], [], []
+    for i in range(gathered, total):
+        source, buffer, kind_count = ins[i], packed[i - gathered], kinds[i - gathered]
+        blocks, tall, columns = buffer.shape
+        size = columns // kind_count
+        for j in range(blocks):
+            for kind in range(kind_count):
+                start = (kind * blocks + j) * size
+                buffer[j, :, kind * size : (kind + 1) * size] = source[:, start : start + size]
+        share = tall >> relays
+        rows = pl.ds(pl.multiple_of((rep % (1 << relays)) * share, share), share)
+        for k, target in enumerate((chip, diagonal)):
+            copy = remote(
+                buffer.at[target, rows],
+                outs[i].at[me, rows],
+                send.at[i, k],
+                recv.at[i, k],
+                "shard",
+                target,
+            )
+            copy.start()
+            shared.append((i, k, target, tall, [copy]))
+        copy = remote(
+            buffer.at[core], outs[i].at[me], send.at[i, 2], recv.at[i, 2], "shard", core
+        )
+        copy.start()
+        whole_copies.append(copy)
+        own = pltpu.make_async_copy(buffer.at[me], outs[i].at[me], local_sem.at[i])
+        own.start()
+        own_copies.append(own)
+    for i in range(late, gathered):
+        begin(i)
+    for i in range(late):
+        pass_on(i)
+    for level, bit in enumerate(bits):
+        for i, k, target, tall, copies in shared:
+            copies[-1].wait_recv()
+            length = (tall >> relays) * bit
+            first = ((rep % (1 << relays)) // bit) * length
+            region = outs[i].at[target, pl.ds(pl.multiple_of(first, length), length)]
+            slot = 3 + 2 * level + k
+            copy = remote(
+                region, region, send.at[i, slot], recv.at[i, slot], "rep", flip(rep, bit)
+            )
+            copy.start()
+            copies.append(copy)
+    for i in range(late, gathered):
+        pass_on(i)
+    for _, _, _, _, copies in shared:
+        copies[-1].wait_recv()
+        for copy in copies:
+            copy.wait_send()
     for far, near, own, relay in pending:
         far.wait_send()
         near.wait()
         own.wait()
         relay.wait()
-    for copies, own in sent:
-        for copy in copies:
-            copy.wait()
-        own.wait()
-
-
-def gather(collective, gathered, swapped, kinds, n_shard):
+    for copy in whole_copies + own_copies:
+        copy.wait()
+
+
+def gather(collective, gathered, swapped, kinds, n_shard, n_rep=1):
     arrays = tuple(gathered) + tuple(swapped)
     shapes = [jax.ShapeDtypeStruct((n_shard,) + a.shape, a.dtype) for a in gathered]
     blocks = [
         jax.ShapeDtypeStruct((n_shard, a.shape[0], a.shape[1] // n_shard), a.dtype)
         for a in swapped
     ]
+    relays = 0
+    if swapped:
+        relays = min(2, n_rep.bit_length() - 1)
+        while relays and any(a.shape[0] % (16 << relays) for a in swapped):
+            relays -= 1
     return pl.pallas_call(
-        functools.partial(gather_kernel, len(gathered), tuple(kinds)),
+        functools.partial(gather_kernel, len(gathered), tuple(kinds), relays),
         out_shape=tuple(shapes + blocks),
         in_specs=[VMEM] * len(arrays),
         out_specs=tuple([VMEM] * len(arrays)),
         scratch_shapes=[pltpu.VMEM(b.shape, b.dtype) for b in blocks]
         + [
-            pltpu.SemaphoreType.DMA((len(arrays), 3)),
-            pltpu.SemaphoreType.DMA((len(arrays), 3)),
+            pltpu.SemaphoreType.DMA((len(arrays), 3 + 2 * relays)),
+            pltpu.SemaphoreType.DMA((len(arrays), 3 + 2 * relays)),
             pltpu.SemaphoreType.DMA((len(arrays),)),
         ],
         compiler_params=pltpu.CompilerParams(collective_id=collective, has_side_effects=True),
@@ -248,7 +292,7 @@
     orders = (low_first, low_first[1::-1] + low_first[2:])
     streams = []
     base = 0
-    for share, order in zip((tiles - tiles // 2, tiles // 2), orders):
+    for share, order in zip((tiles - tiles // 4, tiles // 4), orders):
         if share:
             streams.append(Stream(buffer, base, 16 * share, order, swap))
             base += 16 * share * n_rep
@@ -347,10 +391,11 @@
         _, kept, _, length = self.plans[i][k]
         blocks = range(acc.shape[0]) if stream.swap else (None,)
 
-        @pl.loop(0, length * stream.rows // 16)
+        @pl.loop(0, length)
         def _(p):
-            to = pl.ds(pl.multiple_of(stream.base + kept * stream.rows + 16 * p, 16), 16)
-            of = pl.ds(pl.multiple_of(stream.base + length * stream.rows + 16 * p, 16), 16)
+            to = pl.multiple_of(stream.base + (kept + p) * stream.rows, 16)
+            of = pl.multiple_of(stream.base + (length + p) * stream.rows, 16)
+            to, of = pl.ds(to, stream.rows), pl.ds(of, stream.rows)
             for block in blocks:
                 x, y = ((to,), (of,)) if block is None else ((block, to), (block, of))
                 acc[x] = (acc[x].astype(jnp.float32) + box[y].astype(jnp.float32)).astype(
@@ -407,7 +452,7 @@
             tail = source[t, at : at + half]
             parts.append(jnp.concatenate([tail[:, :rest], tail[:, rest:]], axis=0))
             end += half
-        block = jnp.concatenate([p.astype(jnp.float32) for p in parts], axis=1)
+        block = jnp.concatenate(parts, axis=1)
         gain += source[t, end : end + 16].astype(jnp.float32)
         for kind in range(kinds):
             start = (kind * blocks + t) * size
@@ -436,7 +481,7 @@
         for j in range(out.shape[1] // LANES):
             out[:, j * LANES : (j + 1) * LANES] = source[
                 j * tall + at : j * tall + at + rows
-            ].astype(jnp.float32)
+            ]
         at += rows
 
 
@@ -482,7 +527,9 @@
     outs += [gout.shape, gdown.shape]
     return pl.pallas_call(
         functools.partial(sum_kernel, streams),
-        out_shape=tuple(jax.ShapeDtypeStruct(shape, f32) for shape in outs),
+        out_shape=tuple(
+            jax.ShapeDtypeStruct(shape, f32 if shape == (16, LANES) else b16) for shape in outs
+        ),
         in_specs=[VMEM] * 6,
         out_specs=tuple([VMEM] * 6),
         scratch_shapes=[pltpu.VMEM(shape, b16) for shape in shapes * 3]
@@ -517,6 +564,7 @@
         (qkv_weight, in_weight),
         (3, 2),
         n_shard,
+        n_rep,
     )
     full_g1 = all_g1.reshape(width)
     full_g2 = all_g2.reshape(width)
@@ -610,11 +658,11 @@
         output.reshape(1, tok_dev, width),
         grad_tokens.reshape(1, tok_dev, width),
         sum_g1.reshape(-1)[:part],
-        sum_qkv,
-        sum_out,
+        sum_qkv.astype(f32),
+        sum_out.astype(f32),
         sum_g2.reshape(-1)[:part],
-        sum_in,
-        sum_down,
+        sum_in.astype(f32),
+        sum_down.astype(f32),
     )
 
 

time: 233 us -> 239 us (1.026)
  other arithmetic: 17.1 us -> 23.6 us
  local copies, waits for them, and re-layouts: 21 us -> 14.8 us
  Pallas kernels: 171 us -> 175 us
    pallas_call x1, Pallas kernels: 76.9 us -> 86.6 us  [sum_over_rep(): pl.pallas_call(functools.partial(sum_kernel, streams), out_shape=tuple((j...]
    convert_element_type x0 -> x4, other arithmetic: none -> 6.44 us  [the longest x1 1.98 us: local(): sum_down.astype(f32)]
    unnamed x42 -> x36, local copies, waits for them, and re-layouts: 9.38 us -> 3.1 us
    pallas_call x3, Pallas kernels: 57.9 us -> 52.4 us  [gather(): pl.pallas_call(functools.partial(gather_kernel, len(gathered), tuple(kind...]
where the time goes in v1:
time: 239 us; the launch traced here: 236 us
  Pallas kernels  175 us (73%)
  other arithmetic  23.6 us (10%)
  matrix products  21.7 us (9%)
  local copies, waits for them, and re-layouts  14.8 us (6%)
    pallas_call x1, Pallas kernels, sum_over_rep(): pl.pallas_call(functools.partial(sum_kernel, streams), out_shape=tuple((j...  86.6 us
    pallas_call x3, Pallas kernels, gather(): pl.pallas_call(functools.partial(gather_kernel, len(gathered), tuple(kind...  52.4 us
    pallas_call x3, Pallas kernels, scatter(): pl.pallas_call(functools.partial(scatter_kernel, total), out_shape=tuple(...  36.3 us
    dot_general x4, matrix products, outer_sum(): lax.dot_general(left, right, (((0,), (0,)), ((), ())), preferred_element_...  5.64 us
    dot_general x4, matrix products, times_transposed(): lax.dot_general(left, weight, (((1,), (1,)), ((), ())), preferred_element...  5.59 us

profile of v1, /device:TPU:0, one launch (start us, length us, event | category | flops | bytes accessed | tf_op | source)
XLA Modules:
  0.0 236.4 jit_solution(9688019780623880220)
XLA Ops:
  0.6 1.1 convert_reduce_fusion.1
  1.8 1.2 reshape.284.refs_1_
  3.0 1.2 reshape.285.refs_2_
  4.3 0.9 fusion.46
  5.2 32.1 %shard_map.143 = (bf16[4,128,768]{2,1,0:T(8,128)(2,1)}, bf16[4,1,192]{2,1,0:T(2,128)(2,1)}, bf16[4,1,192]{2,1,0:T(2,128)(2,1)}, bf16[4,128,768]{2,1,0:T(8,128)(2...) custom-call(bf16[128,768]{1,0:T(8,128)(2,1)} %bitcast.112, bf16[1,192]{1,0:T(2,128)(2,1)} %reshape.284.refs_1_, ...), custom_call_target="tpu_custom_call" | custom-call | tf_op jit(solution)/shard_map/pallas_call | solution.py:200
  37.3 0.8 convert_reduce_fusion.2
  38.2 1.3 convert_reduce_fusion
  39.5 1.5 multiply_reduce_fusion.1
  41.1 1.2 fusion.7
  42.6 1.5 copy.16
  44.2 0.7 convolution_bitcast_fusion
  45.0 0.7 copy-done.8
  46.0 0.6 multiply_reduce_fusion
  47.2 1.1 copy-done.1
  48.3 1.4 fusion.42
  49.7 1.3 convolution_convert_fusion.5
  51.0 10.6 %shard_map.144 = f32[128,768]{1,0:T(8,128)} custom-call(bf16[4,128,768]{2,1,0:T(8,128)(2,1)} %bitcast.116), custom_call_target="tpu_custom_call" | custom-call | tf_op jit(solution)/shard_map/pallas_call | solution.py:256
  61.6 1.2 fusion.58
  63.0 0.8 multiply_convert_fusion.4.refs_0_
  63.8 10.2 %shard_map.145 = bf16[4,128,768]{2,1,0:T(8,128)(2,1)} custom-call(bf16[128,768]{1,0:T(8,128)(2,1)} %multiply_convert_fusion.4.refs_0_), custom_call_target="tpu_custom_call" | custom-call | tf_op jit(solution)/shard_map/pallas_call | solution.py:200
  74.0 2.2 fusion.59
  76.2 0.6 fusion.21
  76.8 1.2 convolution_convert_fusion.6.gdown
  78.0 1.7 convolution_convert_fusion.3
  79.7 1.5 convolution_convert_fusion
  81.2 2.2 copy.23
  83.5 1.5 convolution_convert_fusion.4
  84.9 15.2 %shard_map.146 = (f32[128,768]{1,0:T(8,128)}, f32[128,768]{1,0:T(8,128)}) custom-call(bf16[4,128,768]{2,1,0:T(8,128)(2,1)} %bitcast.131, bf16[4,128,768]{2,1,0:T(8,128)(2,1)} %bitcast.129), custom_call_target="tpu_custom_call" | custom-call | tf_op jit(solution)/shard_map/pallas_call | solution.py:256
  100.1 1.2 multiply_reduce_fusion.2
  101.5 2.1 fusion.57
  104.2 10.2 %shard_map.147 = bf16[4,128,768]{2,1,0:T(8,128)(2,1)} custom-call(bf16[128,768]{1,0:T(8,128)(2,1)} %get-tuple-element.42.refs_0_), custom_call_target="tpu_custom_call" | custom-call | tf_op jit(solution)/shard_map/pallas_call | solution.py:200
  114.4 2.3 convolution_convert_fusion.7.gout
  116.7 1.5 convolution_convert_fusion.8
  118.4 0.8 fusion.12
  119.2 1.1 multiply_convert_fusion
  122.5 1.7 convolution_convert_fusion.2
  124.2 0.6 convolution_convert_fusion.1
  124.8 10.6 %shard_map.148 = f32[128,768]{1,0:T(8,128)} custom-call(bf16[4,128,768]{2,1,0:T(8,128)(2,1)} %bitcast.130), custom_call_target="tpu_custom_call" | custom-call | tf_op jit(solution)/shard_map/pallas_call | solution.py:256
  135.4 1.2 fusion.32
  136.8 1.9 fusion.31
  139.3 1.3 copy.22
  140.6 86.6 %shard_map.149 = (bf16[192,2304]{1,0:T(8,128)(2,1)}, f32[16,128]{1,0:T(8,128)}, bf16[192,2304]{1,0:T(8,128)(2,1)}, f32[16,128]{1,0:T(8,128)}, bf16[192,768]{1,0:T(8,128)(2,1)}, /*index=5*/bf16[288,768]{1,0:T(8,128)(2,1)}) custom-call(bf16[4,192,576]{2,1,0:T(8,128)(2,1)} %bitcast.114, bf16[4,16,128]{2,1,0:T(8,128)(2,1)} %pad.19.gain1, ...), custom_call_target="tpu_custom_call" | custom-call | tf_op jit(solution)/shard_map/pallas_call | solution.py:528
  227.2 1.3 slice.74
  228.5 1.2 slice.75
  229.7 1.8 convert_element_type.185
  231.5 2.0 convert_element_type.187
  233.5 1.3 convert_element_type.184
  235.0 1.3 convert_element_type.186
  (70 shorter events, 5.7 us)
Async XLA Ops:
  0.6 75.5 %copy-start = (bf16[288,768]{1,0:T(8,128)(2,1)S(1)}, bf16[288,768]{1,0:T(8,128)(2,1)}, u32[]{:S(2)}) copy-start(bf16[288,768]{1,0:T(8,128)(2,1)} %param.14) | copy-start | bytes 1327108
  37.3 3.8 %copy-start.3 = (bf16[4,128,768]{2,1,0:T(8,128)(2,1)S(1)}, bf16[4,128,768]{2,1,0:T(8,128)(2,1)}, u32[]{:S(2)}) copy-start(bf16[4,128,768]{2,1,0:T(8,128)(2,1)} %get-tuple-element.22) | copy-start | bytes 2359300
  44.8 0.9 copy-start.8
  44.8 1.0 copy-start.10
  46.6 1.7 copy-start.1
  48.3 1.4 copy-start.7
  49.7 11.9 %copy-start.4 = (bf16[1,128,768]{2,1,0:T(8,128)(2,1)S(1)}, bf16[1,128,768]{2,1,0:T(8,128)(2,1)}, u32[]{:S(2)}) copy-start(bf16[1,128,768]{2,1,0:T(8,128)(2,1)} %param.8) | copy-start | bytes 589828
  74.0 2.2 copy-start.17
  76.2 1.8 copy-start.13
  78.0 1.7 copy-start.5
  104.2 14.1 %copy-start.6 = (f32[3,512,64]{1,2,0:T(8,128)S(1)}, f32[3,512,64]{1,2,0:T(8,128)}, u32[]{:S(2)}) copy-start(f32[3,512,64]{1,2,0:T(8,128)} %get-tuple-element.74) | copy-start | bytes 1179652
  114.4 4.0 %copy-start.2 = (f32[3,512,512]{1,2,0:T(8,128)S(1)}, f32[3,512,512]{1,2,0:T(8,128)}, u32[]{:S(2)}) copy-start(f32[3,512,512]{1,2,0:T(8,128)} %copy-done.1) | copy-start | bytes 9437188
  120.8 0.9 copy-start.9
  120.8 1.0 copy-start.11
  121.3 1.2 copy-start.12
  122.5 1.7 copy-start.16
  227.2 6.4 %copy-start.15 = (bf16[192,2304]{1,0:T(8,128)(2,1)S(1)}, bf16[192,2304]{1,0:T(8,128)(2,1)}, u32[]{:S(2)}) copy-start(bf16[192,2304]{1,0:T(8,128)(2,1)} %get-tuple-element.31) | copy-start | bytes 2654212
  233.5 1.5 copy-start.14

commit v2 on v1

--- a/solution.py
+++ b/solution.py
@@ -292,7 +292,7 @@
     orders = (low_first, low_first[1::-1] + low_first[2:])
     streams = []
     base = 0
-    for share, order in zip((tiles - tiles // 4, tiles // 4), orders):
+    for share, order in zip((tiles - tiles // 2, tiles // 2), orders):
         if share:
             streams.append(Stream(buffer, base, 16 * share, order, swap))
             base += 16 * share * n_rep
@@ -406,11 +406,10 @@
         for i in chosen:
             self.begin(i, 0)
 
-    def step(self, chosen, k):
-        for i in chosen:
-            self.finish(i, k)
-            if k < 2 * self.steps:
-                self.begin(i, k + 1)
+    def step(self, i, k):
+        self.finish(i, k)
+        if k < 2 * self.steps:
+            self.begin(i, k + 1)
 
     def close(self, chosen):
         for i in chosen:
@@ -431,9 +430,26 @@
             target[s, at : at + half, :rest] = source[s, :half, full * LANES :]
             target[s, at : at + half, rest:] = source[s, half:, full * LANES :]
             at += half
-        target[s, at : at + 16] = gain[s]
-        if at + 16 < target.shape[1]:
-            target[s, at + 16 :] = jnp.zeros((target.shape[1] - at - 16, LANES), target.dtype)
+        if gain is not None:
+            target[s, at : at + 16] = gain[s]
+            at += 16
+        if at < target.shape[1]:
+            target[s, at:] = jnp.zeros((target.shape[1] - at, LANES), target.dtype)
+
+
+def pack_gain(gain, target, at):
+    blocks = target.shape[0]
+    part = gain.shape[1] // blocks
+    row = lax.broadcasted_iota(jnp.int32, (16, LANES), 0)
+    for s in range(blocks):
+        tile = jnp.zeros((16, LANES), jnp.float32)
+        for j in range(-(-part // LANES)):
+            piece = gain[:, s * part + j * LANES : s * part + min((j + 1) * LANES, part)]
+            room = LANES - piece.shape[1]
+            if room:
+                piece = jnp.concatenate([piece, jnp.zeros((1, room), jnp.float32)], axis=1)
+            tile = jnp.where(row == j, jnp.broadcast_to(piece, (16, LANES)), tile)
+        target[s, at : at + 16] = tile.astype(target.dtype)
 
 
 def unpack_columns(source, out, gain_out, kinds):
@@ -490,50 +506,87 @@
     return rows * columns // LANES + 16
 
 
-def sum_kernel(streams, qkv, gain1, win, gain2, gout, gdown, *refs):
-    o_qkv, o_gain1, o_in, o_gain2, o_out, o_down = refs[:6]
-    acc, box, res = refs[6:9], refs[9:12], refs[12:15]
+def sum_kernel(streams, early, qkv, h1_part, normed, win, gain2, gout, gdown, *refs):
+    o_qkv, o_gain1, o_in, o_gain2, o_out, o_down, o_h1 = refs[:7]
+    acc, box, res = refs[7:10], refs[10:13], refs[13:16]
+    near_buf, out_buf, far_buf, h1_send, h1_recv = refs[16:21]
+    rep_sum = RepSum(streams, acc, box, res, refs[21:])
+    me = rep_sum.me
+    core, chip = flip(me, 1), flip(me, 2)
+    bits = sorted(streams[0].order)
+    greet([("rep", flip(rep_sum.rep, bit)) for bit in bits] + rep_sum.group)
+    first = [
+        remote(
+            h1_part.at[target], near_buf.at[j], h1_send.at[j], h1_recv.at[j], "shard", core
+        )
+        for j, target in enumerate((flip(core, 2), core))
+    ]
+    for copy in first:
+        copy.start()
     pack_rows((gout, gdown), acc[0])
     pack_columns(win, acc[1], gain2)
-    pack_columns(qkv, acc[2], gain1)
-    rep_sum = RepSum(streams, acc, box, res, refs[15:])
-    bits = sorted(streams[0].order)
-    greet([("rep", flip(rep_sum.rep, bit)) for bit in bits] + rep_sum.group)
-    chosen = range(len(streams))
-    rep_sum.begin_all(chosen)
-    for k in range(2 * rep_sum.steps + 1):
-        rep_sum.step(chosen, k)
+    rep_sum.begin_all(range(early))
+    first[0].wait_recv()
+    out_buf[...] = (
+        h1_part[chip].astype(jnp.float32) + near_buf[0].astype(jnp.float32)
+    ).astype(jnp.bfloat16)
+    last = remote(out_buf, far_buf, h1_send.at[2], h1_recv.at[2], "shard", chip)
+    last.start()
+    pack_columns(qkv, acc[2], None)
+    first[1].wait_recv()
+    own = h1_part[me].astype(jnp.float32) + near_buf[1].astype(jnp.float32)
+    last.wait_recv()
+    grad_h1 = own + far_buf[...].astype(jnp.float32)
+    o_h1[...] = grad_h1
+    gain = jnp.sum(grad_h1 * normed[...], axis=0, keepdims=True)
+    pack_gain(gain, acc[2], column_rows(qkv.shape) - 16)
+    rep_sum.begin_all(range(early, len(streams)))
+    pairs = len(streams) // 2
+    for t in range(2 * rep_sum.steps + 1 + pairs):
+        for i in range(len(streams)):
+            k = t - i // 2
+            if 0 <= k <= 2 * rep_sum.steps:
+                rep_sum.step(i, k)
+    for copy in first + [last]:
+        copy.wait_send()
     unpack_rows(res[0], (o_out, o_down))
     unpack_columns(res[1], o_in, o_gain2, 2)
     unpack_columns(res[2], o_qkv, o_gain1, 3)
-    rep_sum.close(chosen)
-
-
-def sum_over_rep(collective, n_rep, qkv, gain1, win, gain2, gout, gdown):
+    rep_sum.close(range(len(streams)))
+
+
+def sum_over_rep(collective, n_rep, qkv, h1_part, normed, win, gain2, gout, gdown):
     b16, f32 = jnp.bfloat16, jnp.float32
     n_shard, part, columns = qkv.shape
     width = columns * n_shard
     plain_rows = (gout.shape[0] + gdown.shape[0]) * gout.shape[1] // LANES
-    streams, shapes = [], []
+    streams, shapes, early = [], [], 0
     for i, (rows, swap) in enumerate(
         ((plain_rows, False), (column_rows(win.shape), True), (column_rows(qkv.shape), True))
     ):
         more, padded = streams_of(i, rows, n_rep, swap)
+        early = len(streams)
         streams += more
         shapes.append((n_shard, padded, LANES) if swap else (padded, LANES))
     steps = len(streams[0].order)
     count = len(streams)
     outs = [(part, width), (16, LANES), (part, win.shape[2] * n_shard), (16, LANES)]
-    outs += [gout.shape, gdown.shape]
+    outs += [gout.shape, gdown.shape, normed.shape]
+    wide = ((16, LANES), normed.shape)
     return pl.pallas_call(
-        functools.partial(sum_kernel, streams),
+        functools.partial(sum_kernel, streams, early),
         out_shape=tuple(
-            jax.ShapeDtypeStruct(shape, f32 if shape == (16, LANES) else b16) for shape in outs
+            jax.ShapeDtypeStruct(shape, f32 if shape in wide else b16) for shape in outs
         ),
-        in_specs=[VMEM] * 6,
-        out_specs=tuple([VMEM] * 6),
+        in_specs=[VMEM] * 7,
+        out_specs=tuple([VMEM] * 7),
         scratch_shapes=[pltpu.VMEM(shape, b16) for shape in shapes * 3]
         + [
+            pltpu.VMEM((2,) + normed.shape, b16),
+            pltpu.VMEM(normed.shape, b16),
+            pltpu.VMEM(normed.shape, b16),
+            pltpu.SemaphoreType.DMA((3,)),
+            pltpu.SemaphoreType.DMA((3,)),
             pltpu.SemaphoreType.DMA((count, 2 * steps)),
             pltpu.SemaphoreType.DMA((count, 2 * steps)),
             pltpu.SemaphoreType.DMA((count, 3)),
@@ -541,7 +594,7 @@
             pltpu.SemaphoreType.DMA((count,)),
         ],
         compiler_params=pltpu.CompilerParams(collective_id=collective, has_side_effects=True),
-    )(qkv, gain1, win, gain2, gout, gdown)
+    )(qkv, h1_part, normed, win, gain2, gout, gdown)
 
 
 def local(
@@ -634,26 +687,25 @@
     ).astype(b16)
     grad_qkv = outer_sum(hidden_one, grad_projected)
     h1_part = times_transposed(grad_projected, my_qkv).astype(b16)
-    (grad_h1,) = scatter(5, (h1_part.reshape(n_shard, tok_dev, width),))
-    norm_grad_one, grad_gain_one = norm_backward(grad_h1, normed_one, inverse_one, full_g1)
-    grad_tokens = grad_resid + norm_grad_one
-
     def gain_rows(gain):
         room = -part % LANES
         rows = jnp.pad(gain.reshape(n_shard, part), ((0, 0), (0, room)))
         rows = rows.reshape(n_shard, -1, LANES)
         return jnp.pad(rows, ((0, 0), (0, 16 - rows.shape[1]), (0, 0))).astype(b16)
 
-    sum_qkv, sum_g1, sum_in, sum_g2, sum_out, sum_down = sum_over_rep(
+    sum_qkv, sum_g1, sum_in, sum_g2, sum_out, sum_down, grad_h1 = sum_over_rep(
         6,
         n_rep,
         grad_qkv.astype(b16).reshape(n_shard, part, -1),
-        gain_rows(grad_gain_one),
+        h1_part.reshape(n_shard, tok_dev, width),
+        normed_one,
         grad_in.astype(b16).reshape(n_shard, part, -1),
         gain_rows(grad_gain_two),
         grad_out.astype(b16),
         grad_down.astype(b16),
     )
+    norm_grad_one, _ = norm_backward(grad_h1, normed_one, inverse_one, full_g1)
+    grad_tokens = grad_resid + norm_grad_one
     return (
         output.reshape(1, tok_dev, width),
         grad_tokens.reshape(1, tok_dev, width),

time: 239 us -> 212 us (0.89)
  Pallas kernels: 175 us -> 151 us
    pallas_call x1, Pallas kernels: 86.6 us -> 73.2 us  [sum_over_rep(): pl.pallas_call(functools.partial(sum_kernel, streams, early), out_shape=t...]
    pallas_call x3 -> x2, Pallas kernels: 36.3 us -> 25.7 us  [scatter(): pl.pallas_call(functools.partial(scatter_kernel, total), out_shape=tuple(...]
where the time goes in v2:
time: 212 us
  Pallas kernels  151 us (71%)
  other arithmetic  23.4 us (11%)
  matrix products  21.6 us (10%)
  local copies, waits for them, and re-layouts  14.1 us (7%)
    pallas_call x1, Pallas kernels, sum_over_rep(): pl.pallas_call(functools.partial(sum_kernel, streams, early), out_shape=t...  73.2 us
    pallas_call x3, Pallas kernels, gather(): pl.pallas_call(functools.partial(gather_kernel, len(gathered), tuple(kind...  52.5 us
    pallas_call x2, Pallas kernels, scatter(): pl.pallas_call(functools.partial(scatter_kernel, total), out_shape=tuple(...  25.7 us
    dot_general x4, matrix products, outer_sum(): lax.dot_general(left, right, (((0,), (0,)), ((), ())), preferred_element_...  5.64 us
    dot_general x4, matrix products, times_transposed(): lax.dot_general(left, weight, (((1,), (1,)), ((), ())), preferred_element...  5.59 us
    reduce_sum x3, other arithmetic, layer_norm(): mean_row = jnp.mean(values, axis=-1, keepdims=True)  4.27 us

profile of v2, /device:TPU:0, one launch (start us, length us, event | category | flops | bytes accessed | tf_op | source)
XLA Modules:
  0.0 211.5 jit_solution(8531268162590230689)
XLA Ops:
  0.6 1.1 convert_reduce_fusion.1
  1.8 1.1 fusion.24
  2.9 1.2 reshape.276.refs_1_
  4.1 1.2 reshape.277.refs_2_
  5.4 0.9 fusion.37
  6.3 32.1 %shard_map.143 = (bf16[4,128,768]{2,1,0:T(8,128)(2,1)}, bf16[4,1,192]{2,1,0:T(2,128)(2,1)}, bf16[4,1,192]{2,1,0:T(2,128)(2,1)}, bf16[4,128,768]{2,1,0:T(8,128)(2...) custom-call(bf16[128,768]{1,0:T(8,128)(2,1)} %bitcast.114, bf16[1,192]{1,0:T(2,128)(2,1)} %reshape.276.refs_1_, ...), custom_call_target="tpu_custom_call" | custom-call | tf_op jit(solution)/shard_map/pallas_call | solution.py:200
  38.5 0.8 convert_reduce_fusion.2
  39.3 1.3 convert_reduce_fusion
  40.6 1.5 multiply_reduce_fusion.1
  42.2 1.2 fusion.7
  43.7 1.5 copy.16
  45.3 0.6 convolution_bitcast_fusion
  46.1 0.7 copy-done.10
  47.1 0.6 multiply_reduce_fusion
  48.2 1.1 copy-done.1
  49.4 1.4 fusion.33
  50.8 1.3 convolution_convert_fusion.5
  52.1 10.5 %shard_map.144 = f32[128,768]{1,0:T(8,128)} custom-call(bf16[4,128,768]{2,1,0:T(8,128)(2,1)} %bitcast.118), custom_call_target="tpu_custom_call" | custom-call | tf_op jit(solution)/shard_map/pallas_call | solution.py:256
  62.6 1.9 fusion.49
  64.7 0.8 multiply_convert_fusion.4.refs_0_
  65.5 10.2 %shard_map.145 = bf16[4,128,768]{2,1,0:T(8,128)(2,1)} custom-call(bf16[128,768]{1,0:T(8,128)(2,1)} %multiply_convert_fusion.4.refs_0_), custom_call_target="tpu_custom_call" | custom-call | tf_op jit(solution)/shard_map/pallas_call | solution.py:200
  75.7 2.2 %fusion.50 = f32[512,576]{0,1:T(8,128)S(1)} fusion(bf16[512,768]{1,0:T(8,128)(2,1)} %bitcast.120, bf16[768,576]{1,0:T(8,128)(2,1)} %bitcast.126), kind=kOutput, calls=%fused_computation.112 | convolution fusion | flops 452984832 | bytes 2850816 | tf_op jit(solution)/shard_map/dot_general | solution.py:651
  77.9 0.6 fusion.21
  78.5 1.2 convolution_convert_fusion.6.gdown
  79.7 1.7 convolution_convert_fusion.3
  81.4 1.5 convolution_convert_fusion
  82.9 2.2 %copy.23 = bf16[768,576]{1,0:T(8,128)(2,1)} copy(bf16[768,576]{0,1:T(8,128)(2,1)} %convolution_convert_fusion) | data formatting | bytes 1769472 | tf_op jit(solution)/shard_map/convert_element_type | solution.py:702
  85.2 1.5 convolution_convert_fusion.4
  86.6 15.2 %shard_map.146 = (f32[128,768]{1,0:T(8,128)}, f32[128,768]{1,0:T(8,128)}) custom-call(bf16[4,128,768]{2,1,0:T(8,128)(2,1)} %bitcast.132, bf16[4,128,768]{2,1,0:T(8,128)(2,1)} %bitcast.131), custom_call_target="tpu_custom_call" | custom-call | tf_op jit(solution)/shard_map/pallas_call | solution.py:256
  101.8 1.2 multiply_reduce_fusion.3
  103.2 2.1 fusion.48
  105.9 10.2 %shard_map.147 = bf16[4,128,768]{2,1,0:T(8,128)(2,1)} custom-call(bf16[128,768]{1,0:T(8,128)(2,1)} %get-tuple-element.43.refs_0_), custom_call_target="tpu_custom_call" | custom-call | tf_op jit(solution)/shard_map/pallas_call | solution.py:200
  116.1 2.3 %convolution_convert_fusion.7.gout = bf16[192,768]{1,0:T(8,128)(2,1)} fusion(bf16[512,192]{0,1:T(8,128)(2,1)S(1)} %bitcast.123, bf16[512,768]{1,0:T(8,128)(2,1)} %bitcast.112), kind=kOutput, calls=%fused_computation.26 | convolution fusion | flops 151142400 | bytes 1277952 | tf_op jit(solution)/shard_map/dot_general | solution.py:57
  118.5 1.5 convolution_convert_fusion.8
  120.1 0.8 fusion.12
  120.9 1.0 multiply_convert_fusion
  124.2 1.7 convolution_convert_fusion.2
  125.9 0.6 convolution_convert_fusion.1
  126.5 1.3 copy.22
  127.9 73.2 %shard_map.148 = (bf16[192,2304]{1,0:T(8,128)(2,1)}, f32[16,128]{1,0:T(8,128)}, bf16[192,2304]{1,0:T(8,128)(2,1)}, f32[16,128]{1,0:T(8,128)}, bf16[192,768]{1,0:...) custom-call(bf16[4,192,576]{2,1,0:T(8,128)(2,1)} %bitcast.116, bf16[4,128,768]{2,1,0:T(8,128)(2,1)} %bitcast.136, ...), custom_call_target="tpu_custom_call" | custom-call | tf_op jit(solution)/shard_map/pallas_call | solution.py:576
  201.1 1.3 slice.74
  202.4 1.2 slice.75
  203.6 1.2 multiply_reduce_fusion.7
  204.9 2.0 add_bitcast_fusion
  206.9 0.9 convert_element_type.182
  207.7 1.0 convert_element_type.184
  208.7 1.3 convert_element_type.181
  210.2 1.3 convert_element_type.183
  (70 shorter events, 4.9 us)
Async XLA Ops:
  0.6 77.2 %copy-start = (bf16[288,768]{1,0:T(8,128)(2,1)S(1)}, bf16[288,768]{1,0:T(8,128)(2,1)}, u32[]{:S(2)}) copy-start(bf16[288,768]{1,0:T(8,128)(2,1)} %param.14) | copy-start | bytes 1327108
  6.3 39.8 %copy-start.8 = (f32[512,64]{0,1:T(8,128)}, f32[512,64]{0,1:T(8,128)S(1)}, u32[]{:S(2)}) copy-start(f32[512,64]{0,1:T(8,128)S(1)} %get-tuple-element.66) | copy-start | bytes 393220
  38.5 3.8 %copy-start.3 = (bf16[4,128,768]{2,1,0:T(8,128)(2,1)S(1)}, bf16[4,128,768]{2,1,0:T(8,128)(2,1)}, u32[]{:S(2)}) copy-start(bf16[4,128,768]{2,1,0:T(8,128)(2,1)} %get-tuple-element.23) | copy-start | bytes 2359300
  45.9 0.9 copy-start.10
  47.7 1.7 copy-start.1
  49.4 1.4 copy-start.7
  50.8 11.8 %copy-start.4 = (bf16[1,128,768]{2,1,0:T(8,128)(2,1)S(1)}, bf16[1,128,768]{2,1,0:T(8,128)(2,1)}, u32[]{:S(2)}) copy-start(bf16[1,128,768]{2,1,0:T(8,128)(2,1)} %param.8) | copy-start | bytes 589828
  75.7 2.2 %copy-start.17 = (bf16[4,128,768]{2,1,0:T(8,128)(2,1)S(1)}, bf16[4,128,768]{2,1,0:T(8,128)(2,1)}, u32[]{:S(2)}) copy-start(bf16[4,128,768]{2,1,0:T(8,128)(2,1)} %get-tuple-element.28) | copy-start | bytes 2359300
  77.9 1.8 copy-start.13
  79.7 1.7 copy-start.5
  105.9 14.1 %copy-start.6 = (f32[3,512,64]{1,2,0:T(8,128)S(1)}, f32[3,512,64]{1,2,0:T(8,128)}, u32[]{:S(2)}) copy-start(f32[3,512,64]{1,2,0:T(8,128)} %get-tuple-element.75) | copy-start | bytes 1179652
  116.1 4.0 %copy-start.2 = (f32[3,512,512]{1,2,0:T(8,128)S(1)}, f32[3,512,512]{1,2,0:T(8,128)}, u32[]{:S(2)}) copy-start(f32[3,512,512]{1,2,0:T(8,128)} %copy-done.1) | copy-start | bytes 9437188
  122.5 0.9 copy-start.9
  122.5 1.0 copy-start.11
  123.0 1.2 copy-start.12
  124.2 1.7 copy-start.16
  201.1 5.8 %copy-start.19 = (bf16[192,768]{1,0:T(8,128)(2,1)S(1)}, bf16[192,768]{1,0:T(8,128)(2,1)}, u32[]{:S(2)}) copy-start(bf16[192,768]{1,0:T(8,128)(2,1)} %get-tuple-element.34) | copy-start | bytes 884740
  201.1 6.6 %copy-start.18 = (bf16[288,768]{1,0:T(8,128)(2,1)S(1)}, bf16[288,768]{1,0:T(8,128)(2,1)}, u32[]{:S(2)}) copy-start(bf16[288,768]{1,0:T(8,128)(2,1)} %get-tuple-element.37) | copy-start | bytes 1327108
  204.9 3.8 %copy-start.15 = (bf16[192,2304]{1,0:T(8,128)(2,1)S(1)}, bf16[192,2304]{1,0:T(8,128)(2,1)}, u32[]{:S(2)}) copy-start(bf16[192,2304]{1,0:T(8,128)(2,1)} %get-tuple-element.33) | copy-start | bytes 2654212
  208.7 1.5 copy-start.14
